TPU v7x, 32 devices: a whole 2x2x4 slice. The times are simulated.
32 devices in a mesh: group: 2 (over x), ctx: 8 (over z, y), tp: 2 (over core).
Axes of the slice: x: 2, y: 2, z: 4, core: 2. Of those that a mesh axis runs over, the one named last changes fastest.
Arguments:
- query_proj: bfloat16 [2048, 8192], P(('group', 'ctx'), 'tp'), parts along dimension 0, may hold values from -6 to 6
- key_proj: bfloat16 [2048, 8192], P(('group', 'ctx'), 'tp'), parts along dimension 0, may hold values from -6 to 6
- value_proj: bfloat16 [2048, 8192], P(('group', 'ctx'), 'tp'), parts along dimension 0, may hold values from -6 to 6
- genome_ids: int32 [2048], P('group'), parts along dimension 0, may hold values from 0 to 3, never falling along the last dimension, each value on 1 to 512 neighbouring positions
- filters: float32 [512, 128], P('tp'), may hold values from -0.5 to 0.5
- out_weight: bfloat16 [8192, 8192], P('tp', 'ctx'), may hold values from -0.0625 to 0.0625
- out_grad: bfloat16 [2048, 8192], P(('group', 'ctx'), 'tp'), parts along dimension 0, may hold values from -6 to 6
Outputs:
- query_grad: bfloat16 [2048, 8192], P(('group', 'ctx'), 'tp'), parts along dimension 0
- key_grad: bfloat16 [2048, 8192], P(('group', 'ctx'), 'tp'), parts along dimension 0
- value_grad: bfloat16 [2048, 8192], P(('group', 'ctx'), 'tp'), parts along dimension 0
- filter_grad: float32 [1024, 128], P(('group', 'tp')), parts along dimension 0
There are 2 independent parts, one for each index of `group`. A program takes and returns all parts, laid end to end along the dimension named above; an argument that names none is the same for every part. Nothing has to cross between parts.
Inputs may be any that keep to these rules, and one draw needn't show every extreme that they name: `genome_ids`: genome ids never fall along the rows; every genome covers 1 to 512 consecutive rows, and one covers exactly 512.
All inputs are finite; a program needn't handle non-finite values.
Results may differ from a plain program's by a relative error of at most 0.017.
Values may be sent and summed in bfloat16 or wider, within the bound.
A program may use at most 192 MiB of HBM per device.

v0:
```python
import jax
import jax.numpy as jnp
import numpy as np
from jax import lax
from jax.sharding import PartitionSpec as P


def from_behind(array, axis, by):
    length = lax.axis_size(axis)
    pairs = [(i, i + by) for i in range(length) if 0 <= i + by < length]
    return lax.ppermute(array, axis, pairs)


def rounded(source):
    return lax.optimization_barrier(source.astype(jnp.bfloat16)).astype(jnp.float32)


def lag_tables(filt_vals, tap_count):
    row_pos = np.arange(tap_count)[:, None]
    col_pos = np.arange(2 * tap_count)[None, :]
    tables = []
    for offsets in (row_pos + tap_count - col_pos, col_pos - row_pos):
        inside = (offsets >= 0) & (offsets < tap_count)
        picked = jnp.take(filt_vals, np.clip(offsets, 0, tap_count - 1).reshape(-1), axis=1)
        picked = picked.reshape(filt_vals.shape[0], tap_count, 2 * tap_count)
        tables.append(jnp.where(inside[None], picked, jnp.zeros_like(picked)))
    return (tables[0], tables[1])


def fold_lags(product, tap_count):
    group_count = product.shape[0]
    flat = product.reshape(group_count, 2 * tap_count * tap_count)
    flat = jnp.concatenate([flat, jnp.zeros((group_count, tap_count), flat.dtype)], 1)
    skewed = flat.reshape(group_count, tap_count, 2 * tap_count + 1)
    return jnp.flip(jnp.sum(skewed[:, :, 1 : tap_count + 1], axis=1), axis=1)


def per_device(query_proj, key_proj, value_proj, genome_ids, filters, out_weight, out_grad):
    row_count, feature_count = query_proj.shape
    group_local = filters.shape[0]
    chan_count = feature_count // group_local
    tap_count = filters.shape[1]
    first_global = lax.axis_index("ctx") * row_count
    pad_ids = jnp.full((tap_count,), -1, jnp.int32)
    ids_pad = jnp.concatenate([pad_ids, genome_ids, pad_ids])
    key_f32 = key_proj.astype(jnp.float32)
    value_f32 = value_proj.astype(jnp.float32)
    mixed = (key_f32 * value_f32).astype(jnp.bfloat16)
    before = from_behind(mixed, "ctx", 1)
    mixed_ext = jnp.concatenate([before, mixed], 0)
    fwd_table, back_table = lag_tables(filters.astype(jnp.bfloat16), tap_count)
    grad_full = lax.all_gather(out_grad, "tp", axis=1, tiled=True)
    columns = lax.all_to_all(grad_full, "ctx", split_axis=1, concat_axis=0, tiled=True)
    summed = lax.psum_scatter(
        lax.dot_general(
            columns, out_weight, (((1,), (1,)), ((), ())), preferred_element_type=jnp.float32
        ).astype(jnp.bfloat16),
        "ctx",
        scatter_dimension=0,
        tiled=True,
    ).astype(jnp.float32)
    dz_vals = rounded(summed)
    block_index = 0
    first_row = block_index * tap_count
    window = mixed_ext
    ids_rows = lax.dynamic_slice_in_dim(ids_pad, first_global + first_row + tap_count, tap_count)
    ids_prev = lax.dynamic_slice_in_dim(ids_pad, first_global + first_row, 2 * tap_count)
    ids_next = lax.dynamic_slice_in_dim(
        ids_pad, first_global + first_row + tap_count, 2 * tap_count
    )
    same_prev = (ids_rows[:, None] == ids_prev[None, :]).astype(jnp.bfloat16)
    prev_masks = [same_prev]
    next_masks = [(ids_rows[:, None] == ids_next[None, :]).astype(jnp.bfloat16)]
    block_out = jnp.einsum(
        "gtw,wgc->tgc",
        fwd_table * same_prev[None],
        window.reshape(2 * tap_count, group_local, chan_count),
        preferred_element_type=jnp.float32,
    )
    conv_parts = block_out.reshape(tap_count, feature_count)
    query_grad = (dz_vals * conv_parts).astype(jnp.bfloat16)
    grad_conv = (dz_vals * query_proj.astype(jnp.float32)).astype(jnp.bfloat16)
    after = from_behind(grad_conv, "ctx", -1)
    grad_ext = jnp.concatenate([grad_conv, after], 0)
    block_index = 0
    window = mixed_ext.reshape(2 * tap_count, group_local, chan_count)
    grad_window = grad_ext.reshape(2 * tap_count, group_local, chan_count)
    grad_rows = grad_conv.reshape(tap_count, group_local, chan_count)
    block_grad = jnp.einsum(
        "gtw,wgc->tgc",
        back_table * next_masks[block_index][None],
        grad_window,
        preferred_element_type=jnp.float32,
    )
    grad_parts = block_grad.reshape(tap_count, feature_count)
    product = jnp.einsum("tgc,wgc->gtw", grad_rows, window, preferred_element_type=jnp.float32)
    filt_local = fold_lags(product * prev_masks[block_index].astype(jnp.float32)[None], tap_count)
    key_grad = (grad_parts * value_f32).astype(jnp.bfloat16)
    value_grad = (grad_parts * key_f32).astype(jnp.bfloat16)
    filter_grad = lax.psum(filt_local.astype(jnp.bfloat16), "ctx").astype(jnp.float32)
    return (query_grad, key_grad, value_grad, filter_grad)


def solution(mesh):
    in_specs = (
        P(("group", "ctx"), "tp"),
        P(("group", "ctx"), "tp"),
        P(("group", "ctx"), "tp"),
        P("group"),
        P("tp", None),
        P("tp", "ctx"),
        P(("group", "ctx"), "tp"),
    )
    out_specs = (
        P(("group", "ctx"), "tp"),
        P(("group", "ctx"), "tp"),
        P(("group", "ctx"), "tp"),
        P(("group", "tp"), None),
    )
    return jax.shard_map(
        per_device, mesh=mesh, in_specs=in_specs, out_specs=out_specs, check_vma=False
    )
```

profile of v0, /device:TPU:0, one launch (start us, length us, event | category | flops | bytes accessed | tf_op | source)
XLA Modules:
  0.0 785.1 jit_solution(3224054432893824704)
XLA Ops:
  7.2 0.0 all-gather.2.cloned.1.call-start
  7.2 2.3 copy.46
  9.5 0.0 all-gather.2.cloned.1.call-update
  9.5 0.0 reduce-scatter.2.cloned.1.call-start
  9.5 13.9 %all-gather.2.cloned.1.call-done = bf16[128,8192]{0,1:T(8,128)(2,1)} async-done(((bf16[128,4096]{0,1:T(8,128)(2,1)}), bf16[128,8192]{0,1:T(8,128)(2,1)}) %all-gather.2.cloned.1.call-update) | async-done | bytes 2097168 | tf_op jit(solution)/shard_map/all_gather | solution.py:52
  23.4 54.4 %all_to_all.19 = bf16[128,8,1024]{0,2,1:T(8,128)(2,1)S(1)} all-to-all(bf16[128,8,1024]{0,2,1:T(8,128)(2,1)} %bitcast.34), channel_id=1, replica_groups=mesh['group'=2,'ctx'=8,'tp'=2] {'ctx'}, dimensions={1} | all-to-all | bytes 4194304 | tf_op jit(solution)/shard_map/all_to_all | solution.py:53
  77.9 2.7 copy.47
  80.5 14.8 %convolution_convert_fusion = bf16[1024,4096]{1,0:T(8,128)(2,1)} fusion(bf16[1024,1024]{1,0:T(8,128)(2,1)} %bitcast.38, bf16[4096,1024]{1,0:T(8,128)(2,1)} %param.18), kind=kOutput, calls=%fused_computation.16 | convolution fusion | flops 8594128896 | bytes 18874368 | tf_op jit(solution)/shard_map/dot_general | solution.py:55
  95.3 0.0 copy-start.5
  95.3 0.0 reduce-scatter.2.cloned.1.call-update
  95.4 0.0 all-reduce.3.cloned.1.call-start
  95.4 0.7 copy-done.7
  96.1 0.1 copy-done.3
  96.2 0.1 copy.49
  96.4 147.2 %reduce-scatter.2.cloned.1.call-done = bf16[128,4096]{1,0:T(8,128)(2,1)} async-done(((bf16[1024,4096]{1,0:T(8,128)(2,1)}), bf16[128,4096]{1,0:T(8,128)(2,1)}) %reduce-scatter.2.cloned.1.call-update) | async-done | bytes 1048592 | tf_op jit(solution)/shard_map/reduce_scatter | solution.py:54
  243.5 1.5 fusion.13
  245.0 1.3 collective-permute-start.1
  246.4 129.4 %gather_fusion.1 = bf16[32768,256]{1,0:T(8,128)(2,1)} fusion(bf16[256,128]{0,1:T(8,128)(2,1)S(1)} %copy.49, s32[32768]{0:T(1024)S(1)} %broadcast_clamp_fusion), kind=kCustom, calls=%fused_computation.1.clone | custom fusion | bytes 33685504 | tf_op jit(solution)/shard_map/jit(_take)/gather | solution.py:24
  375.8 23.5 %copy.53 = bf16[256,128,256]{2,1,0:T(8,128)(2,1)} copy(bf16[256,128,256]{0,2,1:T(8,128)(2,1)} %bitcast.29) | data formatting | bytes 33554432 | tf_op jit(solution)/shard_map/reshape | solution.py:25
  399.3 0.1 dynamic_slice.9
  399.4 0.1 fusion.20
  399.5 0.1 fusion.17
  399.6 0.0 collective-permute-done.1
  399.6 1.4 pad_maximum_fusion.1
  401.0 2.5 copy.52
  403.4 12.2 %fusion = f32[256,16,128]{2,1,0:T(8,128)} fusion(bf16[256,256,16]{0,2,1:T(8,128)(2,1)} %bitcast.35, bf16[256,128,256]{2,1,0:T(8,128)(2,1)} %copy.53, pred[128,256]{1,0:T(8,128)(4,1)S(1)} %copy.61, bf16[128,256]{1,0:T(8,128)(2,1)S(1)} %get-tuple-element.16), kind=kOutput, calls=%fused_computation.4 | convolution fusion | flops 285212672 | bytes 21069824 | tf_op jit(solution)/shard_map/gtw,wgc->tgc/dot_general | solution.py:89
  415.6 1.9 copy.54
  417.6 0.0 copy-start.6
  417.6 0.0 copy-start.4
  417.6 3.7 fusion.14
  421.3 5.5 collective-permute-start
  426.9 129.4 %gather_fusion = bf16[32768,256]{1,0:T(8,128)(2,1)} fusion(bf16[256,128]{0,1:T(8,128)(2,1)S(1)} %copy.49, s32[32768]{0:T(1024)S(1)} %broadcast_clamp_fusion.1), kind=kCustom, calls=%fused_computation.clone | custom fusion | bytes 33685504 | tf_op jit(solution)/shard_map/jit(_take)/gather | solution.py:24
  556.4 23.5 %copy.50 = bf16[256,128,256]{2,1,0:T(8,128)(2,1)} copy(bf16[256,128,256]{0,2,1:T(8,128)(2,1)} %bitcast.28) | data formatting | bytes 33554432 | tf_op jit(solution)/shard_map/reshape | solution.py:25
  579.8 0.7 copy.56
  580.5 3.1 pad_maximum_fusion
  583.6 3.3 copy.48
  586.9 11.6 %fusion.3 = f32[256,16,128]{2,1,0:T(8,128)} fusion(bf16[256,256,16]{0,2,1:T(8,128)(2,1)S(1)} %bitcast.30, bf16[256,128,256]{2,1,0:T(8,128)(2,1)} %copy.50, pred[128,256]{1,0:T(8,128)(4,1)S(1)} %copy.62, bf16[128,256]{1,0:T(8,128)(2,1)S(1)} %get-tuple-element.15), kind=kOutput, calls=%fused_computation.7 | convolution fusion | flops 285212672 | bytes 21069824 | tf_op jit(solution)/shard_map/gtw,wgc->tgc/dot_general | solution.py:74
  598.5 3.0 copy.51
  601.5 13.1 %broadcast_multiply_fusion = f32[256,128,256]{2,1,0:T(8,128)} fusion(f32[128,256]{1,0:T(8,128)S(1)} %get-tuple-element.14, bf16[128,256,16]{0,2,1:T(8,128)(2,1)S(1)} %bitcast.33, bf16[256,256,16]{0,2,1:T(8,128)(2,1)S(1)} %bitcast.31), kind=kOutput, calls=%fused_computation.3 | convolution fusion | flops 276824064 | bytes 36831232 | tf_op jit(solution)/shard_map/tgc,wgc->gtw/dot_general | solution.py:96
  614.6 35.0 %copy.59 = f32[256,128,256]{0,2,1:T(8,128)} copy(f32[256,128,256]{2,1,0:T(8,128)} %broadcast_multiply_fusion) | data formatting | bytes 67108864 | tf_op jit(solution)/shard_map/reshape | solution.py:32
  649.6 22.4 %concatenate.15 = f32[256,32896]{0,1:T(8,128)} pad(f32[256,32768]{0,1:T(8,128)} %bitcast.27, f32[]{:T(128)} %constant.38.clone.1), padding=0_0x0_128 | pad | bytes 67239936 | tf_op jit(solution)/shard_map/concatenate | solution.py:33
  672.0 28.3 %reshape.129 = f32[256,128,257]{0,2,1:T(8,128)} reshape(f32[256,32896]{0,1:T(8,128)} %concatenate.15) | data formatting | bytes 67371008 | tf_op jit(solution)/shard_map/reshape | solution.py:34
  700.3 8.4 %slice_reduce_fusion = bf16[256,128]{0,1:T(8,128)(2,1)S(1)} fusion(f32[256,128,257]{0,2,1:T(8,128)} %reshape.129), kind=kLoop, calls=%fused_computation.2 | loop fusion | flops 4161536 | bytes 16842752 | tf_op jit(solution)/shard_map/reduce_sum | solution.py:35
  708.6 0.7 rev.4
  709.3 0.0 all-reduce.3.cloned.1.call-update
  709.3 1.2 fusion.12
  710.5 66.4 %all-reduce.3.cloned.1.call-done = bf16[256,128]{0,1:T(8,128)(2,1)} async-done(((bf16[256,128]{0,1:T(8,128)(2,1)}), bf16[256,128]{0,1:T(8,128)(2,1)}) %all-reduce.3.cloned.1.call-update) | async-done | bytes 65552 | tf_op jit(solution)/shard_map/psum | solution.py:100
  776.9 1.6 copy.58
  (20 shorter events, 0.1 us)
Async XLA Ops:
  7.2 16.3 %all-gather.2.cloned.1.call-start = ((), (), s32[]{:S(2)}) async-start(), calls=%async_computation.2 | async-start | bytes 3145728 | tf_op jit(solution)/shard_map/all_gather | solution.py:52
  9.5 234.0 %reduce-scatter.2.cloned.1.call-start = ((), (), s32[]{:S(2)}) async-start(), calls=%async_computation.3 | async-start | bytes 9437184 | tf_op jit(solution)/shard_map/reduce_scatter | solution.py:54
  95.3 0.8 copy-start.7
  95.3 0.9 copy-start.3
  95.3 148.2 %copy-start.2 = (bf16[128,4096]{1,0:T(8,128)(2,1)S(1)}, bf16[128,4096]{1,0:T(8,128)(2,1)}, u32[]{:S(2)}) copy-start(bf16[128,4096]{1,0:T(8,128)(2,1)} %param.13) | copy-start | bytes 3145732
  95.3 151.0 %copy-start.5 = (s32[32768]{0:T(1024)S(1)}, s32[32768]{0:T(1024)}, u32[]{:S(2)}) copy-start(s32[32768]{0:T(1024)} %constant.66) | copy-start | bytes 393220
  95.4 681.6 %all-reduce.3.cloned.1.call-start = ((), (), s32[]{:S(2)}) async-start(), calls=%async_computation.4 | async-start | bytes 131072 | tf_op jit(solution)/shard_map/psum | solution.py:100
  245.0 154.6 %collective-permute-start.1 = (bf16[128,4096]{1,0:T(8,128)(2,1)S(1)}, bf16[128,4096]{1,0:T(8,128)(2,1)}, u32[]{:S(2)}, u32[]{:S(2)}) collective-permute-start(bf16[128,4096]{1,0:T(8,128)(2,1)S(1)} %fusion.13), channel_id=1, source_target_pairs={{2,0},{4,2},{6,4},{8,6},{10,8},{12,10},{14,12},{3,1},{5,3},{7,5},{... | collective-permute-start | bytes 3145736 | tf_op jit(solution)/shard_map/ppermute | solution.py:11
  375.8 23.5 %copy-start.8 = (s32[1024]{0:T(1024)S(1)}, s32[1024]{0:T(1024)}, u32[]{:S(2)}) copy-start(s32[1024]{0:T(1024)} %param.16) | copy-start | bytes 12292
  417.6 9.3 %copy-start.6 = (pred[128,256]{1,0:T(32,128)(4,1)S(1)}, pred[128,256]{1,0:T(32,128)(4,1)}, u32[]{:S(2)}) copy-start(pred[128,256]{1,0:T(32,128)(4,1)} %constant.45) | copy-start | bytes 98308
  417.6 9.3 %copy-start.4 = (s32[32768]{0:T(1024)S(1)}, s32[32768]{0:T(1024)}, u32[]{:S(2)}) copy-start(s32[32768]{0:T(1024)} %constant.65) | copy-start | bytes 393220
  421.3 159.2 %collective-permute-start = (bf16[128,4096]{1,0:T(8,128)(2,1)}, bf16[128,4096]{1,0:T(8,128)(2,1)}, u32[]{:S(2)}, u32[]{:S(2)}) collective-permute-start(bf16[128,4096]{1,0:T(8,128)(2,1)} %get-tuple-element.11), channel_id=1, source_target_pairs={{0,2},{2,4},{4,6},{6,8},{8,10},{10,12},{12,14},{1,3},{3,5},{5,7},{... | collective-permute-start | bytes 3145736 | tf_op jit(solution)/shard_map/ppermute | solution.py:11
  700.2 9.1 %copy-start = (f32[128,4096]{1,0:T(8,128)S(1)}, f32[128,4096]{1,0:T(8,128)}, u32[]{:S(2)}) copy-start(f32[128,4096]{1,0:T(8,128)} %copy.51) | copy-start | bytes 6291460
  700.2 9.1 %copy-start.1 = (bf16[128,4096]{1,0:T(8,128)(2,1)S(1)}, bf16[128,4096]{1,0:T(8,128)(2,1)}, u32[]{:S(2)}) copy-start(bf16[128,4096]{1,0:T(8,128)(2,1)} %reduce-scatter.2.cloned.1.call-done) | copy-start | bytes 3145732
Sparse Core Ops, SparseCore 0:
  10.1 13.2 all-gather.1
  95.5 148.0 reduce-scatter.1
  709.4 67.4 all-reduce.2
where the time goes:
time: 788 us; the launch traced here: 785 us
  local copies, waits for them, and re-layouts  411 us (52%)
  waiting for transfers between devices  228 us (29%)
  blocking collectives  54.4 us (7%)
  matrix products  51.7 us (7%)
  other arithmetic  19.3 us (2%)
  between operations  13.9 us (2%)
    gather x2, local copies, waits for them, and re-layouts, lag_tables(): jnp.take(filt_vals, np.clip(offsets, 0, tap_count - 1).reshape(-1), axis=1)  259 us
    reduce_scatter x1, waiting for transfers between devices, per_device(): lax.psum_scatter(lax.dot_general(columns, out_weight, (((1,), (1,)), ((),...  147 us
    psum x1, waiting for transfers between devices, per_device(): lax.psum(filt_local.astype(jnp.bfloat16), 'ctx').astype(jnp.float32)  66.4 us
    all_to_all x1, blocking collectives, per_device(): lax.all_to_all(grad_full, 'ctx', split_axis=1, concat_axis=0, tiled=True)  54.4 us
    reshape x2, local copies, waits for them, and re-layouts, lag_tables(): picked = picked.reshape(filt_vals.shape[0], tap_count, 2 * tap_count)  47 us
    reshape x1, local copies, waits for them, and re-layouts, fold_lags(): flat = product.reshape(group_count, 2 * tap_count * tap_count)  35 us
    reshape x1, local copies, waits for them, and re-layouts, fold_lags(): skewed = flat.reshape(group_count, tap_count, 2 * tap_count + 1)  28.3 us
    concatenate x1, local copies, waits for them, and re-layouts, fold_lags(): jnp.concatenate([flat, jnp.zeros((group_count, tap_count), flat.dtype)], 1)  22.4 us
  transfers between devices with their start and end apart: 5, of which 3 were waited for; matrix products, arithmetic and copies ran while one was open for 39% of the time, Pallas kernels for 0%

commit v1 on v0

--- a/solution.py
+++ b/solution.py
@@ -97,7 +97,9 @@
     filt_local = fold_lags(product * prev_masks[block_index].astype(jnp.float32)[None], tap_count)
     key_grad = (grad_parts * value_f32).astype(jnp.bfloat16)
     value_grad = (grad_parts * key_f32).astype(jnp.bfloat16)
-    filter_grad = lax.psum(filt_local.astype(jnp.bfloat16), "ctx").astype(jnp.float32)
+    filter_grad = jnp.sum(lax.all_gather(filt_local.astype(jnp.bfloat16), "ctx"), axis=0).astype(
+        jnp.float32
+    )
     return (query_grad, key_grad, value_grad, filter_grad)
 
 

time: 788 us -> 752 us (0.954)
  waiting for transfers between devices: 228 us -> 161 us
  blocking collectives: 54.4 us -> 85.8 us
    psum x1 -> x0, waiting for transfers between devices: 66.4 us -> none  [per_device(): lax.psum(filt_local.astype(jnp.bfloat16), 'ctx').astype(jnp.float32)]
    all_gather x0 -> x1, blocking collectives: none -> 31.4 us  [per_device(): lax.all_gather(filt_local.astype(jnp.bfloat16), 'ctx')]
  transfers between devices with their start and end apart: 5 -> 4, of which waited for: 3 -> 2; matrix products, arithmetic and copies ran while one was open for 39% -> 41% of each run, Pallas kernels for 0% -> 0%
where the time goes in v1:
time: 752 us; the launch traced here: 749 us
  local copies, waits for them, and re-layouts  408 us (54%)
  waiting for transfers between devices  161 us (21%)
  blocking collectives  85.8 us (11%)
  matrix products  51.7 us (7%)
  other arithmetic  21.5 us (3%)
  between operations  14.2 us (2%)
    gather x2, local copies, waits for them, and re-layouts, lag_tables(): jnp.take(filt_vals, np.clip(offsets, 0, tap_count - 1).reshape(-1), axis=1)  258 us
    reduce_scatter x1, waiting for transfers between devices, per_device(): lax.psum_scatter(lax.dot_general(columns, out_weight, (((1,), (1,)), ((),...  147 us
    all_to_all x1, blocking collectives, per_device(): lax.all_to_all(grad_full, 'ctx', split_axis=1, concat_axis=0, tiled=True)  54.4 us
    reshape x2, local copies, waits for them, and re-layouts, lag_tables(): picked = picked.reshape(filt_vals.shape[0], tap_count, 2 * tap_count)  46.6 us
    reshape x1, local copies, waits for them, and re-layouts, fold_lags(): flat = product.reshape(group_count, 2 * tap_count * tap_count)  35 us
    all_gather x1, blocking collectives, per_device(): lax.all_gather(filt_local.astype(jnp.bfloat16), 'ctx')  31.4 us
    reshape x1, local copies, waits for them, and re-layouts, fold_lags(): skewed = flat.reshape(group_count, tap_count, 2 * tap_count + 1)  28.3 us
    concatenate x1, local copies, waits for them, and re-layouts, fold_lags(): jnp.concatenate([flat, jnp.zeros((group_count, tap_count), flat.dtype)], 1)  22.4 us
  transfers between devices with their start and end apart: 4, of which 2 were waited for; matrix products, arithmetic and copies ran while one was open for 41% of the time, Pallas kernels for 0%

profile of v1, /device:TPU:0, one launch (start us, length us, event | category | flops | bytes accessed | tf_op | source)
XLA Modules:
  0.0 749.5 jit_solution(9799485302744497335)
XLA Ops:
  7.2 0.0 all-gather.3.cloned.1.call-start
  7.2 2.3 copy.58
  9.5 0.0 all-gather.3.cloned.1.call-update
  9.5 0.0 reduce-scatter.2.cloned.1.call-start
  9.5 13.9 %all-gather.3.cloned.1.call-done = bf16[128,8192]{0,1:T(8,128)(2,1)} async-done(((bf16[128,4096]{0,1:T(8,128)(2,1)}), bf16[128,8192]{0,1:T(8,128)(2,1)}) %all-gather.3.cloned.1.call-update) | async-done | bytes 2097168 | tf_op jit(solution)/shard_map/all_gather | solution.py:52
  23.4 54.4 %all_to_all.19 = bf16[128,8,1024]{0,2,1:T(8,128)(2,1)S(1)} all-to-all(bf16[128,8,1024]{0,2,1:T(8,128)(2,1)} %bitcast.39), channel_id=1, replica_groups=mesh['group'=2,'ctx'=8,'tp'=2] {'ctx'}, dimensions={1} | all-to-all | bytes 4194304 | tf_op jit(solution)/shard_map/all_to_all | solution.py:53
  77.9 2.6 copy.59
  80.5 14.8 %convolution_convert_fusion = bf16[1024,4096]{1,0:T(8,128)(2,1)} fusion(bf16[1024,1024]{1,0:T(8,128)(2,1)} %bitcast.43, bf16[4096,1024]{1,0:T(8,128)(2,1)} %param.18), kind=kOutput, calls=%fused_computation.16 | convolution fusion | flops 8594128896 | bytes 18874368 | tf_op jit(solution)/shard_map/dot_general | solution.py:55
  95.3 0.0 copy-start.3
  95.3 0.0 reduce-scatter.2.cloned.1.call-update
  95.3 0.7 copy-done.5
  96.1 0.1 copy-done.1
  96.2 0.1 copy.61
  96.3 147.2 %reduce-scatter.2.cloned.1.call-done = bf16[128,4096]{1,0:T(8,128)(2,1)} async-done(((bf16[1024,4096]{1,0:T(8,128)(2,1)}), bf16[128,4096]{1,0:T(8,128)(2,1)}) %reduce-scatter.2.cloned.1.call-update) | async-done | bytes 1048592 | tf_op jit(solution)/shard_map/reduce_scatter | solution.py:54
  243.5 1.5 fusion.13
  245.0 1.3 collective-permute-start.1
  246.3 128.8 %gather_fusion.1 = bf16[32768,256]{1,0:T(8,128)(2,1)} fusion(bf16[256,128]{0,1:T(8,128)(2,1)S(1)} %copy.61, s32[32768]{0:T(1024)S(1)} %broadcast_clamp_fusion), kind=kCustom, calls=%fused_computation.1.clone | custom fusion | bytes 33685504 | tf_op jit(solution)/shard_map/jit(_take)/gather | solution.py:24
  375.1 23.3 %copy.65 = bf16[256,128,256]{2,1,0:T(8,128)(2,1)} copy(bf16[256,128,256]{0,2,1:T(8,128)(2,1)} %bitcast.34) | data formatting | bytes 33554432 | tf_op jit(solution)/shard_map/reshape | solution.py:25
  398.5 0.1 dynamic_slice.9
  398.5 0.1 fusion.20
  398.6 0.1 fusion.17
  398.7 0.0 collective-permute-done.1
  398.7 1.4 pad_maximum_fusion.1
  400.1 2.5 copy.64
  402.6 12.2 %fusion = f32[256,16,128]{2,1,0:T(8,128)} fusion(bf16[256,256,16]{0,2,1:T(8,128)(2,1)} %bitcast.40, bf16[256,128,256]{2,1,0:T(8,128)(2,1)} %copy.65, pred[128,256]{1,0:T(8,128)(4,1)S(1)} %copy.73, bf16[128,256]{1,0:T(8,128)(2,1)S(1)} %get-tuple-element.16), kind=kOutput, calls=%fused_computation.4 | convolution fusion | flops 285212672 | bytes 21069824 | tf_op jit(solution)/shard_map/gtw,wgc->tgc/dot_general | solution.py:89
  414.8 1.9 copy.66
  416.7 0.0 copy-start.4
  416.8 0.0 copy-start.2
  416.8 3.7 fusion.14
  420.5 5.6 collective-permute-start
  426.1 128.8 %gather_fusion = bf16[32768,256]{1,0:T(8,128)(2,1)} fusion(bf16[256,128]{0,1:T(8,128)(2,1)S(1)} %copy.61, s32[32768]{0:T(1024)S(1)} %broadcast_clamp_fusion.1), kind=kCustom, calls=%fused_computation.clone | custom fusion | bytes 33685504 | tf_op jit(solution)/shard_map/jit(_take)/gather | solution.py:24
  554.9 23.3 %copy.62 = bf16[256,128,256]{2,1,0:T(8,128)(2,1)} copy(bf16[256,128,256]{0,2,1:T(8,128)(2,1)} %bitcast.33) | data formatting | bytes 33554432 | tf_op jit(solution)/shard_map/reshape | solution.py:25
  578.2 0.7 copy.68
  578.9 3.1 pad_maximum_fusion
  582.0 3.3 copy.60
  585.3 11.6 %fusion.3 = f32[256,16,128]{2,1,0:T(8,128)} fusion(bf16[256,256,16]{0,2,1:T(8,128)(2,1)S(1)} %bitcast.35, bf16[256,128,256]{2,1,0:T(8,128)(2,1)} %copy.62, pred[128,256]{1,0:T(8,128)(4,1)S(1)} %copy.74, bf16[128,256]{1,0:T(8,128)(2,1)S(1)} %get-tuple-element.15), kind=kOutput, calls=%fused_computation.7 | convolution fusion | flops 285212672 | bytes 21069824 | tf_op jit(solution)/shard_map/gtw,wgc->tgc/dot_general | solution.py:74
  596.9 2.9 copy.63
  599.8 3.0 fusion.12
  602.8 13.1 %broadcast_multiply_fusion = f32[256,128,256]{2,1,0:T(8,128)} fusion(f32[128,256]{1,0:T(8,128)S(1)} %get-tuple-element.14, bf16[128,256,16]{0,2,1:T(8,128)(2,1)S(1)} %bitcast.38, bf16[256,256,16]{0,2,1:T(8,128)(2,1)S(1)} %bitcast.36), kind=kOutput, calls=%fused_computation.3 | convolution fusion | flops 276824064 | bytes 36831232 | tf_op jit(solution)/shard_map/tgc,wgc->gtw/dot_general | solution.py:96
  615.9 35.0 %copy.71 = f32[256,128,256]{0,2,1:T(8,128)} copy(f32[256,128,256]{2,1,0:T(8,128)} %broadcast_multiply_fusion) | data formatting | bytes 67108864 | tf_op jit(solution)/shard_map/reshape | solution.py:32
  650.9 22.4 %concatenate.15 = f32[256,32896]{0,1:T(8,128)} pad(f32[256,32768]{0,1:T(8,128)} %bitcast.32, f32[]{:T(128)} %constant.39.clone.1), padding=0_0x0_128 | pad | bytes 67239936 | tf_op jit(solution)/shard_map/concatenate | solution.py:33
  673.4 28.3 %reshape.129 = f32[256,128,257]{0,2,1:T(8,128)} reshape(f32[256,32896]{0,1:T(8,128)} %concatenate.15) | data formatting | bytes 67371008 | tf_op jit(solution)/shard_map/reshape | solution.py:34
  701.6 8.2 %slice_reduce_fusion = bf16[256,128]{0,1:T(8,128)(2,1)S(1)} fusion(f32[256,128,257]{0,2,1:T(8,128)} %reshape.129), kind=kLoop, calls=%fused_computation.2 | loop fusion | flops 4161536 | bytes 16842752 | tf_op jit(solution)/shard_map/reduce_sum | solution.py:35
  709.9 0.1 rev.4
  710.0 31.4 %all-gather = bf16[2048,128]{0,1:T(8,128)(2,1)S(1)} all-gather(bf16[256,128]{0,1:T(8,128)(2,1)S(1)} %rev.4), channel_id=2, replica_groups=mesh['group'=2,'ctx'=8,'tp'=2] {'ctx'}, dimensions={0}, use_global_device_ids=true | all-gather | bytes 589824 | tf_op jit(solution)/shard_map/all_gather | solution.py:100
  741.4 0.1 copy.72
  741.5 0.4 bitcast_reduce_fusion
  741.9 0.8 copy.70
  (16 shorter events, 0.1 us)
Async XLA Ops:
  7.2 16.3 %all-gather.3.cloned.1.call-start = ((), (), s32[]{:S(2)}) async-start(), calls=%async_computation.2 | async-start | bytes 3145728 | tf_op jit(solution)/shard_map/all_gather | solution.py:52
  9.5 234.0 %reduce-scatter.2.cloned.1.call-start = ((), (), s32[]{:S(2)}) async-start(), calls=%async_computation.3 | async-start | bytes 9437184 | tf_op jit(solution)/shard_map/reduce_scatter | solution.py:54
  95.3 0.8 copy-start.5
  95.3 0.9 copy-start.1
  95.3 148.2 %copy-start = (bf16[128,4096]{1,0:T(8,128)(2,1)S(1)}, bf16[128,4096]{1,0:T(8,128)(2,1)}, u32[]{:S(2)}) copy-start(bf16[128,4096]{1,0:T(8,128)(2,1)} %param.13) | copy-start | bytes 3145732
  95.3 151.0 %copy-start.3 = (s32[32768]{0:T(1024)S(1)}, s32[32768]{0:T(1024)}, u32[]{:S(2)}) copy-start(s32[32768]{0:T(1024)} %constant.67) | copy-start | bytes 393220
  245.0 153.7 %collective-permute-start.1 = (bf16[128,4096]{1,0:T(8,128)(2,1)S(1)}, bf16[128,4096]{1,0:T(8,128)(2,1)}, u32[]{:S(2)}, u32[]{:S(2)}) collective-permute-start(bf16[128,4096]{1,0:T(8,128)(2,1)S(1)} %fusion.13), channel_id=1, source_target_pairs={{2,0},{4,2},{6,4},{8,6},{10,8},{12,10},{14,12},{3,1},{5,3},{7,5},{... | collective-permute-start | bytes 3145736 | tf_op jit(solution)/shard_map/ppermute | solution.py:11
  375.1 23.3 %copy-start.6 = (s32[1024]{0:T(1024)S(1)}, s32[1024]{0:T(1024)}, u32[]{:S(2)}) copy-start(s32[1024]{0:T(1024)} %param.16) | copy-start | bytes 12292
  416.7 9.3 %copy-start.4 = (pred[128,256]{1,0:T(32,128)(4,1)S(1)}, pred[128,256]{1,0:T(32,128)(4,1)}, u32[]{:S(2)}) copy-start(pred[128,256]{1,0:T(32,128)(4,1)} %constant.46) | copy-start | bytes 98308
  416.8 9.3 %copy-start.2 = (s32[32768]{0:T(1024)S(1)}, s32[32768]{0:T(1024)}, u32[]{:S(2)}) copy-start(s32[32768]{0:T(1024)} %constant.66) | copy-start | bytes 393220
  420.5 158.4 %collective-permute-start = (bf16[128,4096]{1,0:T(8,128)(2,1)}, bf16[128,4096]{1,0:T(8,128)(2,1)}, u32[]{:S(2)}, u32[]{:S(2)}) collective-permute-start(bf16[128,4096]{1,0:T(8,128)(2,1)} %get-tuple-element.11), channel_id=1, source_target_pairs={{0,2},{2,4},{4,6},{6,8},{8,10},{10,12},{12,14},{1,3},{3,5},{5,7},{... | collective-permute-start | bytes 3145736 | tf_op jit(solution)/shard_map/ppermute | solution.py:11
Sparse Core Ops, SparseCore 0:
  10.1 13.2 all-gather.2
  95.5 148.0 reduce-scatter.1
